TPU v7x, 32 devices: a whole 2x2x4 slice. The times are simulated.
32 devices in a mesh: dp: 4 (over z), layer: 2 (over x), query: 4 (over y, core).
Axes of the slice: x: 2, y: 2, z: 4, core: 2. Of those that a mesh axis runs over, the one named last changes fastest.
Arguments:
- mantissas: bfloat16 [1024, 2, 4096], P('dp', 'layer'), may hold values from -6 to 6
- exponents: int32 [1024, 2, 32], P('dp', 'layer'), may hold values from -2 to 1
- queries: bfloat16 [1024, 2, 4096], P('query', 'layer'), may hold values from -0.0625 to 0.0625
- doc_ids: int32 [1024], P('dp'), may hold values from 0 to 255, never falling along the last dimension, each value on 1 to 32 neighbouring positions
- owners: int32 [256], replicated, may hold values from 0 to 255, each once
Outputs:
- fisher: float32 [2, 4096, 4096], P('layer', 'dp', 'query')
- doc_scores: float32 [256, 1024], P('dp', 'query')
Inputs may be any that keep to these rules, and one draw needn't show every extreme that they name: `doc_ids`: never falling along the rows; every document has 1 to 32 rows, one exactly 32. `owners`: each slot is taken by exactly one document.
All inputs are finite; a program needn't handle non-finite values.
Results may differ from a plain program's by a relative error of at most 0.0003.
Values may be sent and summed in bfloat16 or wider, within the bound.
A program may use at most 64 MiB of HBM per device.

v0:
```python
import jax
import jax.numpy as jnp
from jax import lax
from jax.sharding import PartitionSpec as P


def dequant(mantissas, exponents):
    scale = jnp.exp2(exponents.astype(jnp.float32)).astype(jnp.bfloat16)
    rows, layers, width = mantissas.shape
    blocks = mantissas.reshape(rows, layers, width // 128, 128) * scale[..., None]
    return blocks.reshape(rows, layers, width)


def local_sums(values, doc_ids, owners):
    row_count = values.shape[0]
    doc_total = owners.shape[0]
    first_doc = doc_ids[0]
    local_ids = doc_ids - first_doc
    positions = jnp.arange(row_count, dtype=jnp.int32)
    member = (local_ids[:, None] == positions[None, :]).astype(jnp.float32)
    summed = lax.dot_general(
        member,
        values,
        (((0,), (0,)), ((), ())),
        precision=lax.Precision.HIGHEST,
        preferred_element_type=jnp.float32,
    )
    doc_index = jnp.minimum(first_doc + positions, doc_total - 1)
    slot_ids = owners[doc_index]
    placed = jnp.zeros((doc_total, values.shape[1]), jnp.float32)
    return placed.at[slot_ids].add(summed)


def per_device(mantissas, exponents, queries, doc_ids, owners):
    grads = dequant(mantissas, exponents)
    rows, layers, width = grads.shape
    col_width = width // lax.axis_size("query")
    col_start = lax.axis_index("query") * col_width
    own_width = width // lax.axis_size("dp")
    total_rows = rows * lax.axis_size("dp")
    slab = grads[:, 0, :]
    columns = lax.dynamic_slice_in_dim(slab, col_start, col_width, 1)
    owned = lax.all_to_all(slab, "dp", split_axis=1, concat_axis=0, tiled=True)

    def add_rows(carry, piece, start, owned=owned):
        return lax.dot_general(
            owned, piece, (((0,), (0,)), ((), ())), preferred_element_type=jnp.float32
        )

    empty = jnp.zeros((own_width, col_width), jnp.float32)
    block = add_rows(empty, lax.all_gather(columns, "dp", axis=0, tiled=True), jnp.int32(0))
    blocks_out = [block * (1.0 / total_rows)]
    fisher = jnp.stack(blocks_out, 0)
    flat_grads = grads.reshape(rows, layers * width)
    flat_queries = queries.reshape(queries.shape[0], layers * width)
    scores = lax.dot_general(
        flat_grads, flat_queries, (((1,), (1,)), ((), ())), preferred_element_type=jnp.float32
    )
    summed = lax.psum(scores, "layer")
    doc_terms = local_sums(summed, doc_ids, owners)
    doc_scores = lax.psum_scatter(doc_terms, "dp", scatter_dimension=0, tiled=True)
    return (fisher, doc_scores)


def solution(mesh):
    in_specs = (
        P("dp", "layer", None),
        P("dp", "layer", None),
        P("query", "layer", None),
        P("dp"),
        P(),
    )
    out_specs = (P("layer", "dp", "query"), P("dp", "query"))
    return jax.shard_map(
        per_device, mesh=mesh, in_specs=in_specs, out_specs=out_specs, check_vma=False
    )
```

profile of v0, /device:TPU:0, one launch (start us, length us, event | category | flops | bytes accessed | tf_op | source)
XLA Modules:
  0.0 136.3 jit_solution(11222985315580635377)
XLA Ops:
  8.0 0.0 all-reduce.2.cloned.1.call-start
  8.1 0.9 fusion.8
  9.0 1.4 %mul.37 = bf16[256,32,128]{0,2,1:T(8,128)(2,1)} broadcast(bf16[256,32]{0,1:T(8,128)(2,1)S(1)} %fusion.8), dimensions={0,1} | broadcast | bytes 2113536 | tf_op jit(solution)/shard_map/mul | solution.py:10
  10.4 4.1 %copy.12 = bf16[256,1,4096]{2,0,1:T(8,128)(2,1)} copy(bf16[256,1,4096]{0,2,1:T(8,128)(2,1)} %bitcast.26) | data formatting | bytes 4194304 | tf_op jit(solution)/shard_map/mul | solution.py:10
  14.5 3.7 %fusion = f32[256,256]{1,0:T(8,128)} fusion(bf16[256,1,4096]{2,0,1:T(8,128)(2,1)S(1)} %copy-done, bf16[256,1,4096]{2,0,1:T(8,128)(2,1)} %param.5, bf16[256,1,4096]{2,0,1:T(8,128)(2,1)} %copy.12), kind=kOutput, calls=%fused_computation.3 | convolution fusion | flops 537919488 | bytes 6553600 | tf_op jit(solution)/shard_map/dot_general | solution.py:56
  18.2 0.0 all-gather.2.cloned.1.call-start
  18.3 1.1 constant_dynamic-slice_fusion
  19.3 0.2 copy.13
  19.6 2.1 %dynamic-slice_multiply_fusion = bf16[256,1024]{1,0:T(8,128)(2,1)} fusion(bf16[256,1024]{1,0:T(8,128)(2,1)S(1)} %copy.13, bf16[256,4096]{1,0:T(8,128)(2,1)} %bitcast.29, s32[]{:T(128)S(6)} %select_n.23), kind=kLoop, calls=%fused_computation.8 | loop fusion | flops 1048576 | bytes 1572868 | tf_op jit(solution)/shard_map/mul | solution.py:10
  21.6 0.0 all-gather.2.cloned.1.call-update
  21.6 4.1 %copy.9 = bf16[256,1,4096]{0,2,1:T(8,128)(2,1)} copy(bf16[256,1,4096]{2,0,1:T(8,128)(2,1)} %param.5) | data formatting | bytes 4194304 | tf_op args[0]
  25.7 3.8 %bitcast_multiply_fusion = bf16[256,4,1024]{0,2,1:T(8,128)(2,1)} fusion(bf16[256,4,1024]{0,2,1:T(8,128)(2,1)} %bitcast.30, bf16[256,4,1024]{0,2,1:T(8,128)(2,1)} %bitcast.28), kind=kLoop, calls=%fused_computation.6 | loop fusion | flops 1048576 | bytes 6291456 | tf_op jit(solution)/shard_map/mul | solution.py:10
  29.5 6.4 %all-to-all-start = ((bf16[256,4,1024]{0,2,1:T(8,128)(2,1)}), bf16[256,4,1024]{0,2,1:T(8,128)(2,1)}, u32[]{:S(2)}, u32[]{:S(2)}) async-start(bf16[256,4,1024]{0,2,1:T(8,128)(2,1)} %bitcast_multiply_fusion), calls=%async_computation | async-start | bytes 4194304 | tf_op jit(solution)/shard_map/all_to_all | solution.py:43
  36.0 0.5 slice.3
  36.5 0.7 compare_select_fusion.1
  37.1 1.9 %gather_fusion = s32[256]{0:T(256)S(1)} fusion(s32[256]{0:T(256)S(1)} %copy-done.1, s32[1024]{0:T(1024)S(1)} %pad_clamp_fusion), kind=kCustom, calls=%fused_computation | custom fusion | bytes 3072 | tf_op jit(solution)/shard_map/gather | solution.py:29
  39.1 0.7 broadcast_subtract_fusion
  39.8 4.6 %all-reduce.2.cloned.1.call-done = f32[256,256]{1,0:T(8,128)} async-done(((f32[256,256]{1,0:T(8,128)}), f32[256,256]{1,0:T(8,128)}) %all-reduce.2.cloned.1.call-update) | async-done | bytes 262160 | tf_op jit(solution)/shard_map/psum | solution.py:59
  44.4 1.4 %fusion.4 = f32[256,256]{1,0:T(8,128)S(1)} fusion(f32[256,256]{1,0:T(8,128)} %all-reduce.2.cloned.1.call-done, s32[256]{0:T(256)S(1)} %broadcast_subtract_fusion), kind=kOutput, calls=%fused_computation.10 | convolution fusion | flops 201392128 | bytes 525312 | tf_op jit(solution)/shard_map/dot_general | solution.py:21
  45.8 2.6 %scatter_custom_fusion = f32[256,256]{1,0:T(8,128)} fusion(s32[256]{0:T(256)S(1)} %bitcast.34, f32[256,256]{1,0:T(8,128)S(1)} %fusion.4, f32[]{:T(128)} %constant.5.clone.1), kind=kCustom, calls=%fused_computation.12 | custom fusion | flops 65536 | bytes 262148 | tf_op jit(solution)/shard_map/scatter-add | solution.py:31
  48.4 66.3 %all-to-all-done = bf16[256,4,1024]{0,2,1:T(8,128)(2,1)} async-done(((bf16[256,4,1024]{0,2,1:T(8,128)(2,1)}), bf16[256,4,1024]{0,2,1:T(8,128)(2,1)}, u32[]{:S(2)}, u32[]{:S(2)}) %all-to-all-start) | async-done | bytes 2097184 | tf_op jit(solution)/shard_map/all_to_all | solution.py:43
  114.7 4.0 %copy.10 = bf16[4,256,1024]{2,1,0:T(8,128)(2,1)} copy(bf16[4,256,1024]{1,2,0:T(8,128)(2,1)} %bitcast.3) | data formatting | bytes 4194304 | tf_op jit(solution)/shard_map/all_to_all | solution.py:43
  118.8 6.6 %multiply_bitcast_fusion = f32[1,1024,1024]{2,1,0:T(8,128)} fusion(bf16[1024,1024]{1,0:T(8,128)(2,1)} %bitcast.31, bf16[1024,1024]{1,0:T(8,128)(2,1)} %all-gather.2.cloned.1.call-done), kind=kOutput, calls=%fused_computation.2 | convolution fusion | flops 2148532224 | bytes 8388608 | tf_op jit(solution)/shard_map/dot_general | solution.py:46
  125.4 3.4 %reduce-scatter.2.cloned.1.call-done = f32[64,256]{1,0:T(8,128)} async-done(((f32[256,256]{1,0:T(8,128)}), f32[64,256]{1,0:T(8,128)}) %reduce-scatter.2.cloned.1.call-update) | async-done | bytes 65552 | tf_op jit(solution)/shard_map/reduce_scatter | solution.py:61
  (12 shorter events, 0.1 us)
Async XLA Ops:
  8.0 6.5 %copy-start = (bf16[256,1,4096]{2,0,1:T(8,128)(2,1)S(1)}, bf16[256,1,4096]{2,0,1:T(8,128)(2,1)}, u32[]{:S(2)}) copy-start(bf16[256,1,4096]{2,0,1:T(8,128)(2,1)} %param.7) | copy-start | bytes 6291460
  8.0 36.3 %all-reduce.2.cloned.1.call-start = ((), (), s32[]{:S(2)}) async-start(), calls=%async_computation.3 | async-start | bytes 524288 | tf_op jit(solution)/shard_map/psum | solution.py:59
  18.2 100.6 %all-gather.2.cloned.1.call-start = ((), (), s32[]{:S(2)}) async-start(), calls=%async_computation.2 | async-start | bytes 2621440 | tf_op jit(solution)/shard_map/all_gather | solution.py:51
  29.5 6.4 %copy-start.2 = (s32[256]{0:T(256)S(1)}, s32[256]{0:T(256)}, u32[]{:S(2)}) copy-start(s32[256]{0:T(256)} %param.8) | copy-start | bytes 3076
  29.5 7.6 %copy-start.1 = (s32[256]{0:T(256)S(1)}, s32[256]{0:T(256)}, u32[]{:S(2)}) copy-start(s32[256]{0:T(256)} %param.9) | copy-start | bytes 3076
  29.5 85.2 %all-to-all-start = ((bf16[256,4,1024]{0,2,1:T(8,128)(2,1)}), bf16[256,4,1024]{0,2,1:T(8,128)(2,1)}, u32[]{:S(2)}, u32[]{:S(2)}) async-start(bf16[256,4,1024]{0,2,1:T(8,128)(2,1)} %bitcast_multiply_fusion), calls=%async_computation | async-start | bytes 4194304 | tf_op jit(solution)/shard_map/all_to_all | solution.py:43
  35.9 92.9 %reduce-scatter.2.cloned.1.call-start = ((), (), s32[]{:S(2)}) async-start(), calls=%async_computation.4 | async-start | bytes 327680 | tf_op jit(solution)/shard_map/reduce_scatter | solution.py:61
Sparse Core Ops, SparseCore 0:
  18.3 25.9 all-reduce.1
Sparse Core Ops, SparseCore 1:
  21.7 86.0 all-gather.1
  110.4 18.3 reduce-scatter.1
where the time goes:
time: 137 us; the launch traced here: 136 us
  waiting for transfers between devices  74.4 us (54%)
  local copies, waits for them, and re-layouts  17.4 us (13%)
  between operations  15.6 us (11%)
  matrix products  11.7 us (9%)
  other arithmetic  10.7 us (8%)
  starting transfers between devices  6.52 us (5%)
    all_to_all x1, waiting for transfers between devices, per_device(): owned = lax.all_to_all(slab, 'dp', split_axis=1, concat_axis=0, tiled=True)  66.3 us
    mul x3, other arithmetic, dequant(): mantissas.reshape(rows, layers, width // 128, 128) * scale[..., None]  6.76 us
    dot_general x1, matrix products, add_rows(): lax.dot_general(owned, piece, (((0,), (0,)), ((), ())), preferred_element...  6.63 us
    all_to_all x1, starting transfers between devices, per_device(): owned = lax.all_to_all(slab, 'dp', split_axis=1, concat_axis=0, tiled=True)  6.43 us
    mul x2, local copies, waits for them, and re-layouts, dequant(): mantissas.reshape(rows, layers, width // 128, 128) * scale[..., None]  5.51 us
    psum x1, waiting for transfers between devices, per_device(): summed = lax.psum(scores, 'layer')  4.59 us
    unnamed x8, local copies, waits for them, and re-layouts  4.3 us
    all_to_all x1, local copies, waits for them, and re-layouts, per_device(): owned = lax.all_to_all(slab, 'dp', split_axis=1, concat_axis=0, tiled=True)  4.03 us
  transfers between devices with their start and end apart: 4, of which 3 were waited for; matrix products, arithmetic and copies ran while one was open for 22% of the time, Pallas kernels for 0%

commit v1 on v0

v1 whole, which is shorter than its diff:
```python
import functools

import jax
import jax.numpy as jnp
from jax import lax
from jax.experimental import pallas as pl
from jax.experimental.pallas import tpu as pltpu
from jax.sharding import PartitionSpec as P

MESH = pl.DeviceIdType.MESH
LANES = 128


def remote(src, dst, send, recv, **target):
    return pltpu.make_async_remote_copy(
        src_ref=src, dst_ref=dst, send_sem=send, recv_sem=recv,
        device_id=target, device_id_type=MESH,
    )


def scale_columns(exps):
    return jnp.transpose(jnp.exp2(exps.astype(jnp.float32)))


def spread(scale, width=LANES):
    return jnp.broadcast_to(scale, (scale.shape[0], width)).astype(jnp.bfloat16)


def gather_kernel(
    sizes, m_hbm, e_hbm, q_hbm, doc_ref, owner_ref,
    gcol, gown, ecol, eown, ds_out,
    mv, qv, ev, terms, from_layers, part, from_dp, total,
    load_sem, z_send, z_recv, o_send, o_recv, e_send, e_recv, f_send, f_recv,
    x_send, x_recv, s_send, s_recv, r_send, r_recv, out_sem,
):
    n, layers, queries, pieces, own_width = sizes
    rows, width = m_hbm.shape
    col_width = width // queries
    col_blocks = col_width // LANES
    piece = rows // pieces
    d, l, q = (lax.axis_index(a) for a in ("dp", "layer", "query"))
    source = lax.div(d * own_width, col_width)
    offset = pl.multiple_of(lax.rem(d * own_width, col_width), LANES)
    sub = terms.shape[2]

    def other(index, step, size):
        return lax.rem(index + step + size, size)

    loads = [
        pltpu.make_async_copy(e_hbm, ev, load_sem.at[0]),
        pltpu.make_async_copy(m_hbm, mv, load_sem.at[1]),
        pltpu.make_async_copy(q_hbm, qv, load_sem.at[2]),
    ]

    barrier = pltpu.get_barrier_semaphore()
    for name, index, size in (("dp", d, n), ("layer", l, layers), ("query", q, queries)):
        for step in range(1, size):
            pl.semaphore_signal(
                barrier, inc=1, device_id={name: other(index, step, size)}, device_id_type=MESH
            )
    for load in loads:
        load.start()
    pl.semaphore_wait(barrier, n + layers + queries - 3)

    cols = pl.ds(pl.multiple_of(q * col_width, LANES), col_width)
    own_in_col = pl.ds(offset, own_width)

    def z_copy(way, step, c, first):
        block = d - step if way == 0 else d + step
        at = pl.ds(c * piece, piece)
        src = m_hbm.at[at, cols] if first else gcol.at[block, at]
        return remote(
            src, gcol.at[block, at], z_send.at[way, step, c], z_recv.at[way, step, c],
            dp=d + 1 if way == 0 else d - 1,
        )

    def sends(way, step):
        if way == 0:
            return jnp.logical_and(d < n - 1, d - step >= 0)
        return jnp.logical_and(d > 0, d + step <= n - 1)

    def arrives(way, step):
        if way == 0:
            return d - 1 - step >= 0
        return d + 1 + step <= n - 1

    def incoming(way, step):
        return d - 1 - step if way == 0 else d + 1 + step

    for c in range(pieces):
        for way in (0, 1):
            @pl.when(sends(way, 0))
            def _(way=way, c=c):
                z_copy(way, 0, c, True).start()

    e_rows = pl.ds(pl.multiple_of(q * col_blocks, 8), col_blocks)

    def e_copy(step):
        return remote(
            e_hbm.at[e_rows], ecol.at[d], e_send.at[step - 1], e_recv.at[step - 1],
            dp=other(d, step, n),
        )

    for step in range(1, n):
        e_copy(step).start()

    for load in loads:
        load.wait()
    scales = scale_columns(ev[...])
    for j in range(width // LANES):
        at = slice(j * LANES, (j + 1) * LANES)
        mv[:, at] = mv[:, at] * spread(scales[:, j:j + 1])
    scores = jnp.zeros((rows, qv.shape[0]), jnp.float32)
    depth = width // 4
    for j in range(4):
        at = slice(j * depth, (j + 1) * depth)
        scores += lax.dot_general(
            mv[:, at], qv[:, at], (((1,), (1,)), ((), ())), preferred_element_type=jnp.float32
        )
    docs = owner_ref.shape[1]
    slot_of = (
        lax.broadcasted_iota(jnp.int32, (docs, docs), 0) == owner_ref[...]
    ).astype(jnp.float32).astype(jnp.bfloat16)
    doc_of = (
        lax.broadcasted_iota(jnp.int32, (docs, rows), 0) == doc_ref[...]
    ).astype(jnp.float32).astype(jnp.bfloat16)
    member = jnp.dot(slot_of, doc_of, preferred_element_type=jnp.float32).astype(jnp.bfloat16)
    high = scores.astype(jnp.bfloat16)
    rest = scores - high.astype(jnp.float32)
    middle = rest.astype(jnp.bfloat16)
    low = (rest - middle.astype(jnp.float32)).astype(jnp.bfloat16)
    summed = (
        jnp.dot(member, low, preferred_element_type=jnp.float32)
        + jnp.dot(member, middle, preferred_element_type=jnp.float32)
    ) + jnp.dot(member, high, preferred_element_type=jnp.float32)
    terms[...] = summed.reshape(terms.shape)

    def x_copy(step):
        to = other(l, step, layers)
        return remote(
            terms.at[:, to], from_layers.at[step - 1],
            x_send.at[step - 1], x_recv.at[step - 1], layer=to,
        )

    def s_copy(step):
        to = other(d, step, n)
        return remote(
            part.at[to], from_dp.at[step - 1], s_send.at[step - 1], s_recv.at[step - 1], dp=to
        )

    def r_copy(step):
        to = other(l, step, layers)
        return remote(
            total.at[l], total.at[l], r_send.at[step - 1], r_recv.at[step - 1], layer=to
        )

    for step in range(1, layers):
        x_copy(step).start()

    def over_layers():
        for step in range(1, layers):
            x_copy(step).wait_recv()
        value = terms[:, l]
        for step in range(1, layers):
            value = value + from_layers[step - 1]
        part[...] = value
        for step in range(1, n):
            s_copy(step).start()

    def over_dp():
        for step in range(1, n):
            s_copy(step).wait_recv()
        value = part[d]
        for step in range(1, n):
            value = value + from_dp[step - 1]
        total[l] = value
        for step in range(1, layers):
            r_copy(step).start()

    def f_copy(step, to_step):
        block = other(d, -step, n)
        return remote(
            ecol.at[block], eown.at[block], f_send.at[step - 1, to_step - 1], f_recv.at[step - 1],
            query=other(q, to_step, queries),
        )

    def exponents_on():
        for step in range(1, n):
            e_copy(step).wait_recv()

        @pl.when(q == source)
        def _():
            for step in range(1, n):
                for to_step in range(1, queries):
                    f_copy(step, to_step).start()

    core = lax.rem(q, 2)
    source_core = lax.rem(source, 2)
    sibling = q + 1 - 2 * core
    is_source = q == source
    is_relay = jnp.logical_and(q != source, core == source_core)

    def o_copy(way, step, c, k, from_source):
        block = incoming(way, step)
        at = pl.ds(c * piece, piece)
        src = gcol.at[block, at, own_in_col] if from_source else gown.at[block, at]
        to = sibling if k == 0 else other(q, 2 * k, queries)
        return remote(
            src, gown.at[block, at], o_send.at[way, step, c, k], o_recv.at[way, step, c], query=to
        )

    def on_arrival(way, step, c):
        @pl.when(arrives(way, step))
        def _():
            z_copy(way, step, c, False).wait_recv()

            @pl.when(sends(way, step + 1))
            def _():
                z_copy(way, step + 1, c, False).start()

            @pl.when(is_source)
            def _():
                for k in reversed(range(queries // 2)):
                    o_copy(way, step, c, k, True).start()

    def on_own(way, step, c):
        @pl.when(jnp.logical_and(arrives(way, step), q != source))
        def _():
            o_copy(way, step, c, 0, False).wait_recv()

            @pl.when(is_relay)
            def _():
                o_copy(way, step, c, 0, False).start()

    items = [(way, step, c) for step in range(n - 1) for c in range(pieces) for way in (0, 1)]
    lag = 4
    for i in range(len(items) + lag):
        if i < len(items):
            on_arrival(*items[i])
        if i >= lag:
            on_own(*items[i - lag])
        if i == 1:
            over_layers()
        if i == 3:
            exponents_on()
        if i == 5:
            over_dp()

    for step in range(1, layers):
        r_copy(step).wait_recv()
    out = pltpu.make_async_copy(total, ds_out, out_sem)
    out.start()

    @pl.when(q != source)
    def _():
        for step in range(1, n):
            f_copy(step, 1).wait_recv()

    @pl.when(q == source)
    def _():
        for step in range(1, n):
            for to_step in range(1, queries):
                f_copy(step, to_step).wait_send()

    for step in range(1, n):
        e_copy(step).wait_send()
        s_copy(step).wait_send()
    for step in range(1, layers):
        x_copy(step).wait_send()
        r_copy(step).wait_send()
    for way, step, c in items:
        @pl.when(sends(way, step))
        def _(way=way, step=step, c=c):
            z_copy(way, step, c, step == 0).wait_send()

        @pl.when(jnp.logical_and(arrives(way, step), is_source))
        def _(way=way, step=step, c=c):
            for k in range(queries // 2):
                o_copy(way, step, c, k, True).wait_send()

        @pl.when(jnp.logical_and(arrives(way, step), is_relay))
        def _(way=way, step=step, c=c):
            o_copy(way, step, c, 0, False).wait_send()
    out.wait()


def fisher_kernel(
    sizes, m_hbm, e_hbm, gcol, gown, ecol, eown, ds_in, fisher, ds_out,
    cv, ov, ecv, eov, tile, dsv, c_sem, o_sem, ec_sem, eo_sem, t_sem, ds_sem,
):
    n, queries, own_width = sizes
    rows, width = m_hbm.shape
    col_width = width // queries
    col_blocks, own_blocks = col_width // LANES, own_width // LANES
    d, q = lax.axis_index("dp"), lax.axis_index("query")
    source = lax.div(d * own_width, col_width)
    offset = pl.multiple_of(lax.rem(d * own_width, col_width), LANES)
    cols = pl.ds(pl.multiple_of(q * col_width, LANES), col_width)
    owns = pl.ds(pl.multiple_of(d * own_width, LANES), own_width)
    ds_load = pltpu.make_async_copy(ds_in, dsv, ds_sem.at[0])
    ds_store = pltpu.make_async_copy(dsv, ds_out, ds_sem.at[1])

    def c_copy(src, b):
        return pltpu.make_async_copy(src, cv.at[pl.ds(b * rows, rows)], c_sem.at[b])

    def o_copy(src, b):
        return pltpu.make_async_copy(src, ov.at[pl.ds(b * rows, rows)], o_sem.at[b])

    def e_rows(index):
        return e_hbm.at[pl.ds(pl.multiple_of(index * col_blocks, 8), col_blocks)]

    for b in range(n):
        @pl.when(b == d)
        def _(b=b):
            pltpu.make_async_copy(e_rows(q), ecv.at[b], ec_sem.at[b]).start()
            pltpu.make_async_copy(e_rows(source), eov.at[b], eo_sem.at[b]).start()
            c_copy(m_hbm.at[:, cols], b).start()
            o_copy(m_hbm.at[:, owns], b).start()

        @pl.when(b != d)
        def _(b=b):
            pltpu.make_async_copy(ecol.at[b], ecv.at[b], ec_sem.at[b]).start()
            c_copy(gcol.at[b], b).start()

            @pl.when(q == source)
            def _():
                pltpu.make_async_copy(ecol.at[b], eov.at[b], eo_sem.at[b]).start()
                o_copy(gcol.at[b, :, pl.ds(offset, own_width)], b).start()

            @pl.when(q != source)
            def _():
                pltpu.make_async_copy(eown.at[b], eov.at[b], eo_sem.at[b]).start()
                o_copy(gown.at[b], b).start()
    ds_load.start()

    lane = lax.broadcasted_iota(jnp.int32, (rows, col_blocks), 1)
    for b in range(n):
        at_rows = slice(b * rows, (b + 1) * rows)
        pltpu.make_async_copy(ecol.at[b], ecv.at[b], ec_sem.at[b]).wait()
        c_copy(gcol.at[b], b).wait()
        scales = scale_columns(ecv[b])
        for j in range(col_blocks):
            at = slice(j * LANES, (j + 1) * LANES)
            cv[at_rows, at] = cv[at_rows, at] * spread(scales[:, j:j + 1])
        pltpu.make_async_copy(eown.at[b], eov.at[b], eo_sem.at[b]).wait()
        o_copy(gown.at[b], b).wait()
        scales = scale_columns(eov[b])
        for j in range(own_blocks):
            if own_blocks == col_blocks:
                scale = scales[:, j:j + 1]
            else:
                chosen = lane == lax.div(offset, LANES) + j
                scale = jnp.sum(jnp.where(chosen, scales, 0.0), axis=1, keepdims=True)
            at = slice(j * LANES, (j + 1) * LANES)
            ov[at_rows, at] = ov[at_rows, at] * spread(scale)

    ds_load.wait()
    ds_store.start()
    height = tile.shape[1]
    steps = own_width // height

    def t_copy(i):
        return pltpu.make_async_copy(
            tile.at[i], fisher.at[0, pl.ds(pl.multiple_of(i * height, 8), height)], t_sem.at[i]
        )

    def body(i, _):
        at = pl.ds(pl.multiple_of(i * height, LANES), height)
        block = lax.dot_general(
            ov[:, at], cv[...], (((0,), (0,)), ((), ())), preferred_element_type=jnp.float32
        )
        tile[i] = block * (1.0 / (n * rows))
        t_copy(i).start()
        return 0

    lax.fori_loop(0, steps, body, 0)
    for i in range(steps):
        t_copy(i).wait()
    ds_store.wait()


def per_device(mantissas, exponents, queries, doc_ids, owners):
    n, layers, nq = (lax.axis_size(a) for a in ("dp", "layer", "query"))
    rows, _, width = mantissas.shape
    m = mantissas.reshape(rows, width)
    e = jnp.transpose(exponents[:, 0, :])
    qs = queries.reshape(queries.shape[0], width)
    docs = owners.shape[0]
    own_width, col_width = width // n, width // nq
    col_blocks = col_width // LANES
    slots = docs // n
    sub = slots // layers
    pieces = max(1, 16 // n)
    count = qs.shape[0]
    f32, bf16 = jnp.float32, jnp.bfloat16
    dma = pltpu.SemaphoreType.DMA
    anyspace = pl.BlockSpec(memory_space=pl.ANY)
    vmem = pl.BlockSpec(memory_space=pltpu.VMEM)
    gcol, gown, ecol, eown, ds = pl.pallas_call(
        functools.partial(gather_kernel, (n, layers, nq, pieces, own_width)),
        out_shape=(
            jax.ShapeDtypeStruct((n, rows, col_width), bf16),
            jax.ShapeDtypeStruct((n, rows, own_width), bf16),
            jax.ShapeDtypeStruct((n, col_blocks, rows), jnp.int32),
            jax.ShapeDtypeStruct((n, col_blocks, rows), jnp.int32),
            jax.ShapeDtypeStruct((layers, sub, count), f32),
        ),
        in_specs=[anyspace, anyspace, anyspace, vmem, vmem],
        out_specs=(anyspace,) * 5,
        scratch_shapes=[
            pltpu.VMEM((rows, width), bf16),
            pltpu.VMEM((count, width), bf16),
            pltpu.VMEM(e.shape, jnp.int32),
            pltpu.VMEM((n, layers, sub, count), f32),
            pltpu.VMEM((layers - 1, n, sub, count), f32),
            pltpu.VMEM((n, sub, count), f32),
            pltpu.VMEM((n - 1, sub, count), f32),
            pltpu.VMEM((layers, sub, count), f32),
            dma((3,)),
            dma((2, n - 1, pieces)),
            dma((2, n - 1, pieces)),
            dma((2, n - 1, pieces, nq // 2)),
            dma((2, n - 1, pieces)),
            dma((n - 1,)),
            dma((n - 1,)),
            dma((n - 1, nq - 1)),
            dma((n - 1,)),
            dma((layers - 1,)),
            dma((layers - 1,)),
            dma((n - 1,)),
            dma((n - 1,)),
            dma((layers - 1,)),
            dma((layers - 1,)),
            dma,
        ],
        compiler_params=pltpu.CompilerParams(
            collective_id=0, has_side_effects=True, vmem_limit_bytes=32 * 2**20
        ),
        name="gather",
    )(m, e, qs, doc_ids.reshape(1, rows), owners.reshape(1, docs))
    height = min(256, own_width)
    steps = own_width // height
    fisher, ds = pl.pallas_call(
        functools.partial(fisher_kernel, (n, nq, own_width)),
        out_shape=(
            jax.ShapeDtypeStruct((1, own_width, col_width), f32),
            jax.ShapeDtypeStruct((layers, sub, count), f32),
        ),
        in_specs=[anyspace] * 7,
        out_specs=(anyspace, anyspace),
        scratch_shapes=[
            pltpu.VMEM((n * rows, col_width), bf16),
            pltpu.VMEM((n * rows, own_width), bf16),
            pltpu.VMEM((n, col_blocks, rows), jnp.int32),
            pltpu.VMEM((n, col_blocks, rows), jnp.int32),
            pltpu.VMEM((steps, height, col_width), f32),
            pltpu.VMEM((layers, sub, count), f32),
            dma((n,)),
            dma((n,)),
            dma((n,)),
            dma((n,)),
            dma((steps,)),
            dma((2,)),
        ],
        compiler_params=pltpu.CompilerParams(vmem_limit_bytes=48 * 2**20),
        name="fisher",
    )(m, e, gcol, gown, ecol, eown, ds)
    return fisher, ds.reshape(slots, count)


def solution(mesh):
    in_specs = (
        P("dp", "layer", None),
        P("dp", "layer", None),
        P("query", "layer", None),
        P("dp"),
        P(),
    )
    out_specs = (P("layer", "dp", "query"), P("dp", "query"))
    return jax.shard_map(
        per_device, mesh=mesh, in_specs=in_specs, out_specs=out_specs, check_vma=False
    )
```

time: 137 us -> 62.3 us (0.45)
  the two profiles are of different devices: /device:TPU:0 before, /device:TPU:5 now
where the time goes in v1:
time: 62.3 us; the launch traced here: 62.1 us
  Pallas kernels  54.8 us (88%)
  local copies, waits for them, and re-layouts  6.63 us (11%)
  between operations  0.66 us (1%)
    pallas_call x1, Pallas kernels, per_device(): pl.pallas_call(functools.partial(gather_kernel, (n, layers, nq, pieces, o...  47.5 us
    pallas_call x1, Pallas kernels, per_device(): pl.pallas_call(functools.partial(fisher_kernel, (n, nq, own_width)), out_...  7.31 us
    unnamed x16, local copies, waits for them, and re-layouts  6.63 us

profile of v1, /device:TPU:5, one launch (start us, length us, event | category | flops | bytes accessed | tf_op | source)
XLA Modules:
  0.0 62.1 jit_solution(4983348658631176257)
XLA Ops:
  0.6 0.0 copy-start
  0.6 1.6 %copy-done = bf16[256,1,4096]{2,0,1:T(8,128)(2,1)S(1)} copy-done((bf16[256,1,4096]{2,0,1:T(8,128)(2,1)S(1)}, bf16[256,1,4096]{2,0,1:T(8,128)(2,1)}, u32[]{:S(2)}) %copy-start) | copy-done | bytes 2097176
  2.2 0.0 copy-start.3
  2.2 1.6 %copy-done.3 = bf16[256,1,4096]{2,0,1:T(8,128)(2,1)S(1)} copy-done((bf16[256,1,4096]{2,0,1:T(8,128)(2,1)S(1)}, bf16[256,1,4096]{2,0,1:T(8,128)(2,1)}, u32[]{:S(2)}) %copy-start.3) | copy-done | bytes 2097176
  3.8 0.0 copy-start.4
  3.8 0.8 %copy-done.4 = s32[256,1,32]{0,2,1:T(8,128)S(1)} copy-done((s32[256,1,32]{0,2,1:T(8,128)S(1)}, s32[256,1,32]{0,2,1:T(8,128)}, u32[]{:S(2)}) %copy-start.4) | copy-done | bytes 32792
  4.6 0.0 copy-start.6
  4.6 0.7 %copy-done.6 = s32[256]{0:T(256)S(1)} copy-done((s32[256]{0:T(256)S(1)}, s32[256]{0:T(256)}, u32[]{:S(2)}) %copy-start.6) | copy-done | bytes 1048
  5.3 0.0 copy-start.7
  5.3 0.7 %copy-done.7 = s32[256]{0:T(256)S(1)} copy-done((s32[256]{0:T(256)S(1)}, s32[256]{0:T(256)}, u32[]{:S(2)}) %copy-start.7) | copy-done | bytes 1048
  5.9 0.0 copy-start.1
  5.9 0.0 copy-start.5
  5.9 47.5 %gather.1 = (bf16[4,256,1024]{2,1,0:T(8,128)(2,1)S(1)}, bf16[4,256,1024]{2,1,0:T(8,128)(2,1)S(1)}, s32[4,8,256]{2,1,0:T(8,128)S(1)}, s32[4,8,256]{2,1,0:T(8,128)S(1)}, f32[2,32,256]{2,1,0:T(8,128)S(1)}) custom-call(bf16[256,4096]{1,0:T(8,128)(2,1)S(1)} %bitcast.8, s32[32,256]{1,0:T(8,128)S(1)} %bitcast.11, bf16[256,4096]{1,0:T(8,128)(2,1)S(1)} %bitcast.10, ...), custom_call_target="tpu_custom_call" | custom-call | tf_op jit(solution)/shard_map/gather/pallas_call | solution.py:399
  53.4 0.0 copy-start.2
  53.4 1.3 %copy-done.2 = bf16[4,256,1024]{2,1,0:T(8,128)(2,1)} copy-done((bf16[4,256,1024]{2,1,0:T(8,128)(2,1)}, bf16[4,256,1024]{2,1,0:T(8,128)(2,1)S(1)}, u32[]{:S(2)}) %copy-start.2) | copy-done | bytes 2097176
  54.8 0.0 copy-done.1
  54.8 0.0 copy-done.5
  54.8 7.3 %fisher.1 = (f32[1,1024,1024]{2,1,0:T(8,128)}, f32[2,32,256]{2,1,0:T(8,128)}) custom-call(bf16[256,4096]{1,0:T(8,128)(2,1)S(1)} %bitcast.9, s32[32,256]{1,0:T(8,128)S(1)} %bitcast.12, bf16[4,256,1024]{2,1,0:T(8,128)(2,1)S(1)} %get-tuple-element.9.gcol, bf16[4,256,1024]{2,1,0:T(8,128)(2,1)} %copy-done.2, s32[4,8,256]{2,1,0:T(8,128)S(1)} %get-tuple-element.11.ecol, ...), custom_call_target="tpu_custom_call" | custom-call | tf_op jit(solution)/shard_map/fisher/pallas_call | solution.py:443
Async XLA Ops:
  0.6 1.6 %copy-start = (bf16[256,1,4096]{2,0,1:T(8,128)(2,1)S(1)}, bf16[256,1,4096]{2,0,1:T(8,128)(2,1)}, u32[]{:S(2)}) copy-start(bf16[256,1,4096]{2,0,1:T(8,128)(2,1)} %param.5) | copy-start | bytes 6291460
  2.2 1.6 %copy-start.3 = (bf16[256,1,4096]{2,0,1:T(8,128)(2,1)S(1)}, bf16[256,1,4096]{2,0,1:T(8,128)(2,1)}, u32[]{:S(2)}) copy-start(bf16[256,1,4096]{2,0,1:T(8,128)(2,1)} %param.7) | copy-start | bytes 6291460
  3.8 0.8 %copy-start.4 = (s32[256,1,32]{0,2,1:T(8,128)S(1)}, s32[256,1,32]{0,2,1:T(8,128)}, u32[]{:S(2)}) copy-start(s32[256,1,32]{0,2,1:T(8,128)} %param.6) | copy-start | bytes 98308
  4.6 0.7 %copy-start.6 = (s32[256]{0:T(256)S(1)}, s32[256]{0:T(256)}, u32[]{:S(2)}) copy-start(s32[256]{0:T(256)} %param.8) | copy-start | bytes 3076
  5.3 0.7 %copy-start.7 = (s32[256]{0:T(256)S(1)}, s32[256]{0:T(256)}, u32[]{:S(2)}) copy-start(s32[256]{0:T(256)} %param.9) | copy-start | bytes 3076
  5.9 48.8 %copy-start.1 = (bf16[256,1,4096]{2,0,1:T(8,128)(2,1)S(1)}, bf16[256,1,4096]{2,0,1:T(8,128)(2,1)}, u32[]{:S(2)}) copy-start(bf16[256,1,4096]{2,0,1:T(8,128)(2,1)} %param.5) | copy-start | bytes 6291460
  5.9 48.8 %copy-start.5 = (s32[256,1,32]{0,2,1:T(8,128)S(1)}, s32[256,1,32]{0,2,1:T(8,128)}, u32[]{:S(2)}) copy-start(s32[256,1,32]{0,2,1:T(8,128)} %param.6) | copy-start | bytes 98308
  53.4 1.3 %copy-start.2 = (bf16[4,256,1024]{2,1,0:T(8,128)(2,1)}, bf16[4,256,1024]{2,1,0:T(8,128)(2,1)S(1)}, u32[]{:S(2)}) copy-start(bf16[4,256,1024]{2,1,0:T(8,128)(2,1)S(1)} %get-tuple-element.10.gown) | copy-start | bytes 6291460

commit v2 on v1

--- a/solution.py
+++ b/solution.py
@@ -27,10 +27,11 @@
 
 
 def gather_kernel(
-    sizes, m_hbm, e_hbm, q_hbm, doc_ref, owner_ref,
-    gcol, gown, ecol, eown, ds_out,
-    mv, qv, ev, terms, from_layers, part, from_dp, total,
-    load_sem, z_send, z_recv, o_send, o_recv, e_send, e_recv, f_send, f_recv,
+    sizes, m_hbm, e_hbm, q_hbm, doc_hbm, owner_hbm,
+    acc_out, col_out, own_out, ds_out,
+    gcol, gown, ecol, eown, dcol, down, acc,
+    mv, qv, ev, doc_ref, owner_ref, terms, from_layers, part, from_dp, total,
+    load_sem, l_sem, z_send, z_recv, o_send, o_recv, e_send, e_recv, f_send, f_recv,
     x_send, x_recv, s_send, s_recv, r_send, r_recv, out_sem,
 ):
     n, layers, queries, pieces, own_width = sizes
@@ -50,6 +51,8 @@
         pltpu.make_async_copy(e_hbm, ev, load_sem.at[0]),
         pltpu.make_async_copy(m_hbm, mv, load_sem.at[1]),
         pltpu.make_async_copy(q_hbm, qv, load_sem.at[2]),
+        pltpu.make_async_copy(doc_hbm, doc_ref, load_sem.at[3]),
+        pltpu.make_async_copy(owner_hbm, owner_ref, load_sem.at[4]),
     ]
 
     barrier = pltpu.get_barrier_semaphore()
@@ -157,6 +160,25 @@
     for step in range(1, layers):
         x_copy(step).start()
 
+    height = min(256, own_width)
+
+    def add_block(own_of, col, first):
+        def body(i, _):
+            at = pl.ds(pl.multiple_of(i * height, LANES), height)
+            block = lax.dot_general(
+                own_of(i * height), col[...], (((0,), (0,)), ((), ())),
+                preferred_element_type=jnp.float32,
+            )
+            acc[at] = block if first else acc[at] + block
+            return 0
+
+        lax.fori_loop(0, own_width // height, body, 0)
+
+    add_block(
+        lambda start: mv[:, pl.ds(pl.multiple_of(d * own_width + start, LANES), height)],
+        mv.at[:, cols], True,
+    )
+
     def over_layers():
         for step in range(1, layers):
             x_copy(step).wait_recv()
@@ -194,6 +216,11 @@
                 for to_step in range(1, queries):
                     f_copy(step, to_step).start()
 
+        @pl.when(q != source)
+        def _():
+            for step in range(1, n):
+                f_copy(step, 1).wait_recv()
+
     core = lax.rem(q, 2)
     source_core = lax.rem(source, 2)
     sibling = q + 1 - 2 * core
@@ -223,14 +250,70 @@
                 for k in reversed(range(queries // 2)):
                     o_copy(way, step, c, k, True).start()
 
+    last = jnp.where(d >= (n + 1) // 2, 0, n - 1)
+    own_blocks = own_width // LANES
+    acc_copy = pltpu.make_async_copy(acc, acc_out, l_sem.at[0, 0])
+
+    def last_copies(way, c):
+        at = pl.ds(c * piece, piece)
+        return (
+            pltpu.make_async_copy(dcol.at[way, at], col_out.at[at], l_sem.at[1, c]),
+            pltpu.make_async_copy(down.at[way, at], own_out.at[at], l_sem.at[2, c]),
+        )
+
     def on_own(way, step, c):
-        @pl.when(jnp.logical_and(arrives(way, step), q != source))
+        @pl.when(arrives(way, step))
         def _():
-            o_copy(way, step, c, 0, False).wait_recv()
-
-            @pl.when(is_relay)
+            block = incoming(way, step)
+            at = pl.ds(c * piece, piece)
+            here = slice(c * piece, (c + 1) * piece)
+            scales = scale_columns(ecol[block])[here]
+            for j in range(col_blocks):
+                lanes = slice(j * LANES, (j + 1) * LANES)
+                dcol[way, at, lanes] = gcol[block, at, lanes] * spread(scales[:, j:j + 1])
+
+            def own_piece(source_ref, base):
+                scales = scale_columns(
+                    ecol[block] if source_ref is gcol else eown[block]
+                )[here]
+                lane = lax.broadcasted_iota(jnp.int32, scales.shape, 1)
+                for j in range(own_blocks):
+                    if own_blocks == col_blocks:
+                        scale = scales[:, j:j + 1]
+                    else:
+                        chosen = lane == lax.div(offset, LANES) + j
+                        scale = jnp.sum(jnp.where(chosen, scales, 0.0), axis=1, keepdims=True)
+                    from_lanes = pl.ds(pl.multiple_of(base + j * LANES, LANES), LANES)
+                    down[way, at, j * LANES:(j + 1) * LANES] = (
+                        source_ref[block, at, from_lanes] * spread(scale)
+                    )
+
+            @pl.when(q == source)
             def _():
-                o_copy(way, step, c, 0, False).start()
+                own_piece(gcol, offset)
+
+            @pl.when(q != source)
+            def _():
+                o_copy(way, step, c, 0, False).wait_recv()
+
+                @pl.when(is_relay)
+                def _():
+                    o_copy(way, step, c, 0, False).start()
+
+                own_piece(gown, 0)
+
+            @pl.when(block == last)
+            def _():
+                for copy in last_copies(way, c):
+                    copy.start()
+
+            if c == pieces - 1:
+                @pl.when(block != last)
+                def _():
+                    add_block(
+                        lambda start: down[way, :, pl.ds(pl.multiple_of(start, LANES), height)],
+                        dcol.at[way], False,
+                    )
 
     items = [(way, step, c) for step in range(n - 1) for c in range(pieces) for way in (0, 1)]
     lag = 4
@@ -246,15 +329,11 @@
         if i == 5:
             over_dp()
 
+    acc_copy.start()
     for step in range(1, layers):
         r_copy(step).wait_recv()
     out = pltpu.make_async_copy(total, ds_out, out_sem)
     out.start()
-
-    @pl.when(q != source)
-    def _():
-        for step in range(1, n):
-            f_copy(step, 1).wait_recv()
 
     @pl.when(q == source)
     def _():
@@ -281,83 +360,17 @@
         @pl.when(jnp.logical_and(arrives(way, step), is_relay))
         def _(way=way, step=step, c=c):
             o_copy(way, step, c, 0, False).wait_send()
+    for c in range(pieces):
+        for copy in last_copies(0, c):
+            copy.wait()
+    acc_copy.wait()
     out.wait()
 
 
-def fisher_kernel(
-    sizes, m_hbm, e_hbm, gcol, gown, ecol, eown, ds_in, fisher, ds_out,
-    cv, ov, ecv, eov, tile, dsv, c_sem, o_sem, ec_sem, eo_sem, t_sem, ds_sem,
-):
-    n, queries, own_width = sizes
-    rows, width = m_hbm.shape
-    col_width = width // queries
-    col_blocks, own_blocks = col_width // LANES, own_width // LANES
-    d, q = lax.axis_index("dp"), lax.axis_index("query")
-    source = lax.div(d * own_width, col_width)
-    offset = pl.multiple_of(lax.rem(d * own_width, col_width), LANES)
-    cols = pl.ds(pl.multiple_of(q * col_width, LANES), col_width)
-    owns = pl.ds(pl.multiple_of(d * own_width, LANES), own_width)
-    ds_load = pltpu.make_async_copy(ds_in, dsv, ds_sem.at[0])
-    ds_store = pltpu.make_async_copy(dsv, ds_out, ds_sem.at[1])
-
-    def c_copy(src, b):
-        return pltpu.make_async_copy(src, cv.at[pl.ds(b * rows, rows)], c_sem.at[b])
-
-    def o_copy(src, b):
-        return pltpu.make_async_copy(src, ov.at[pl.ds(b * rows, rows)], o_sem.at[b])
-
-    def e_rows(index):
-        return e_hbm.at[pl.ds(pl.multiple_of(index * col_blocks, 8), col_blocks)]
-
-    for b in range(n):
-        @pl.when(b == d)
-        def _(b=b):
-            pltpu.make_async_copy(e_rows(q), ecv.at[b], ec_sem.at[b]).start()
-            pltpu.make_async_copy(e_rows(source), eov.at[b], eo_sem.at[b]).start()
-            c_copy(m_hbm.at[:, cols], b).start()
-            o_copy(m_hbm.at[:, owns], b).start()
-
-        @pl.when(b != d)
-        def _(b=b):
-            pltpu.make_async_copy(ecol.at[b], ecv.at[b], ec_sem.at[b]).start()
-            c_copy(gcol.at[b], b).start()
-
-            @pl.when(q == source)
-            def _():
-                pltpu.make_async_copy(ecol.at[b], eov.at[b], eo_sem.at[b]).start()
-                o_copy(gcol.at[b, :, pl.ds(offset, own_width)], b).start()
-
-            @pl.when(q != source)
-            def _():
-                pltpu.make_async_copy(eown.at[b], eov.at[b], eo_sem.at[b]).start()
-                o_copy(gown.at[b], b).start()
-    ds_load.start()
-
-    lane = lax.broadcasted_iota(jnp.int32, (rows, col_blocks), 1)
-    for b in range(n):
-        at_rows = slice(b * rows, (b + 1) * rows)
-        pltpu.make_async_copy(ecol.at[b], ecv.at[b], ec_sem.at[b]).wait()
-        c_copy(gcol.at[b], b).wait()
-        scales = scale_columns(ecv[b])
-        for j in range(col_blocks):
-            at = slice(j * LANES, (j + 1) * LANES)
-            cv[at_rows, at] = cv[at_rows, at] * spread(scales[:, j:j + 1])
-        pltpu.make_async_copy(eown.at[b], eov.at[b], eo_sem.at[b]).wait()
-        o_copy(gown.at[b], b).wait()
-        scales = scale_columns(eov[b])
-        for j in range(own_blocks):
-            if own_blocks == col_blocks:
-                scale = scales[:, j:j + 1]
-            else:
-                chosen = lane == lax.div(offset, LANES) + j
-                scale = jnp.sum(jnp.where(chosen, scales, 0.0), axis=1, keepdims=True)
-            at = slice(j * LANES, (j + 1) * LANES)
-            ov[at_rows, at] = ov[at_rows, at] * spread(scale)
-
-    ds_load.wait()
-    ds_store.start()
-    height = tile.shape[1]
-    steps = own_width // height
+def fisher_kernel(scale, acc, col, own, ds_in, fisher, ds_out, tile, t_sem, ds_sem):
+    ds_copy = pltpu.make_async_copy(ds_in, ds_out, ds_sem)
+    ds_copy.start()
+    steps, height, _ = tile.shape
 
     def t_copy(i):
         return pltpu.make_async_copy(
@@ -367,16 +380,16 @@
     def body(i, _):
         at = pl.ds(pl.multiple_of(i * height, LANES), height)
         block = lax.dot_general(
-            ov[:, at], cv[...], (((0,), (0,)), ((), ())), preferred_element_type=jnp.float32
-        )
-        tile[i] = block * (1.0 / (n * rows))
+            own[:, at], col[...], (((0,), (0,)), ((), ())), preferred_element_type=jnp.float32
+        )
+        tile[i] = (acc[at] + block) * scale
         t_copy(i).start()
         return 0
 
     lax.fori_loop(0, steps, body, 0)
     for i in range(steps):
         t_copy(i).wait()
-    ds_store.wait()
+    ds_copy.wait()
 
 
 def per_device(mantissas, exponents, queries, doc_ids, owners):
@@ -396,27 +409,37 @@
     dma = pltpu.SemaphoreType.DMA
     anyspace = pl.BlockSpec(memory_space=pl.ANY)
     vmem = pl.BlockSpec(memory_space=pltpu.VMEM)
-    gcol, gown, ecol, eown, ds = pl.pallas_call(
+    hbm = pl.BlockSpec(memory_space=pltpu.HBM)
+    acc, col, own, ds = pl.pallas_call(
         functools.partial(gather_kernel, (n, layers, nq, pieces, own_width)),
         out_shape=(
-            jax.ShapeDtypeStruct((n, rows, col_width), bf16),
-            jax.ShapeDtypeStruct((n, rows, own_width), bf16),
-            jax.ShapeDtypeStruct((n, col_blocks, rows), jnp.int32),
-            jax.ShapeDtypeStruct((n, col_blocks, rows), jnp.int32),
-            jax.ShapeDtypeStruct((layers, sub, count), f32),
+            pltpu.VMEM((own_width, col_width), f32),
+            pltpu.VMEM((rows, col_width), bf16),
+            pltpu.VMEM((rows, own_width), bf16),
+            pltpu.VMEM((layers, sub, count), f32),
         ),
-        in_specs=[anyspace, anyspace, anyspace, vmem, vmem],
-        out_specs=(anyspace,) * 5,
+        in_specs=[hbm] * 5,
+        out_specs=(anyspace,) * 4,
         scratch_shapes=[
+            pltpu.VMEM((n, rows, col_width), bf16),
+            pltpu.VMEM((n, rows, own_width), bf16),
+            pltpu.VMEM((n, col_blocks, rows), jnp.int32),
+            pltpu.VMEM((n, col_blocks, rows), jnp.int32),
+            pltpu.VMEM((2, rows, col_width), bf16),
+            pltpu.VMEM((2, rows, own_width), bf16),
+            pltpu.VMEM((own_width, col_width), f32),
             pltpu.VMEM((rows, width), bf16),
             pltpu.VMEM((count, width), bf16),
             pltpu.VMEM(e.shape, jnp.int32),
+            pltpu.VMEM((1, rows), jnp.int32),
+            pltpu.VMEM((1, docs), jnp.int32),
             pltpu.VMEM((n, layers, sub, count), f32),
             pltpu.VMEM((layers - 1, n, sub, count), f32),
             pltpu.VMEM((n, sub, count), f32),
             pltpu.VMEM((n - 1, sub, count), f32),
             pltpu.VMEM((layers, sub, count), f32),
-            dma((3,)),
+            dma((5,)),
+            dma((3, pieces)),
             dma((2, n - 1, pieces)),
             dma((2, n - 1, pieces)),
             dma((2, n - 1, pieces, nq // 2)),
@@ -434,37 +457,28 @@
             dma,
         ],
         compiler_params=pltpu.CompilerParams(
-            collective_id=0, has_side_effects=True, vmem_limit_bytes=32 * 2**20
+            collective_id=0, has_side_effects=True, vmem_limit_bytes=58 * 2**20
         ),
         name="gather",
     )(m, e, qs, doc_ids.reshape(1, rows), owners.reshape(1, docs))
-    height = min(256, own_width)
+    height = min(128, own_width)
     steps = own_width // height
     fisher, ds = pl.pallas_call(
-        functools.partial(fisher_kernel, (n, nq, own_width)),
+        functools.partial(fisher_kernel, 1.0 / (n * rows)),
         out_shape=(
             jax.ShapeDtypeStruct((1, own_width, col_width), f32),
             jax.ShapeDtypeStruct((layers, sub, count), f32),
         ),
-        in_specs=[anyspace] * 7,
-        out_specs=(anyspace, anyspace),
+        in_specs=[vmem] * 4,
+        out_specs=(hbm, hbm),
         scratch_shapes=[
-            pltpu.VMEM((n * rows, col_width), bf16),
-            pltpu.VMEM((n * rows, own_width), bf16),
-            pltpu.VMEM((n, col_blocks, rows), jnp.int32),
-            pltpu.VMEM((n, col_blocks, rows), jnp.int32),
             pltpu.VMEM((steps, height, col_width), f32),
-            pltpu.VMEM((layers, sub, count), f32),
-            dma((n,)),
-            dma((n,)),
-            dma((n,)),
-            dma((n,)),
             dma((steps,)),
-            dma((2,)),
+            dma,
         ],
-        compiler_params=pltpu.CompilerParams(vmem_limit_bytes=48 * 2**20),
+        compiler_params=pltpu.CompilerParams(vmem_limit_bytes=16 * 2**20),
         name="fisher",
-    )(m, e, gcol, gown, ecol, eown, ds)
+    )(acc, col, own, ds)
     return fisher, ds.reshape(slots, count)
 
 

time: 62.3 us -> 52.8 us (0.85)
  local copies, waits for them, and re-layouts: 6.63 us -> 0 us
  Pallas kernels: 54.8 us -> 52 us
    unnamed x16 -> x0, local copies, waits for them, and re-layouts: 6.63 us -> none
    pallas_call x1, Pallas kernels: 7.31 us -> 3.05 us  [per_device(): pl.pallas_call(functools.partial(fisher_kernel, 1.0 / (n * rows)), out_sh...]
    pallas_call x1, Pallas kernels: 47.5 us -> 48.9 us  [per_device(): pl.pallas_call(functools.partial(gather_kernel, (n, layers, nq, pieces, o...]
where the time goes in v2:
time: 52.8 us; the launch traced here: 52.6 us
  Pallas kernels  52 us (98%)
  between operations  0.64 us (1%)
    pallas_call x1, Pallas kernels, per_device(): pl.pallas_call(functools.partial(gather_kernel, (n, layers, nq, pieces, o...  48.9 us
    pallas_call x1, Pallas kernels, per_device(): pl.pallas_call(functools.partial(fisher_kernel, 1.0 / (n * rows)), out_sh...  3.05 us

profile of v2, /device:TPU:5, one launch (start us, length us, event | category | flops | bytes accessed | tf_op | source)
XLA Modules:
  0.0 52.6 jit_solution(12608832904345995965)
XLA Ops:
  0.6 48.9 %gather.1 = (f32[1024,1024]{1,0:T(8,128)S(1)}, bf16[256,1024]{1,0:T(8,128)(2,1)S(1)}, bf16[256,1024]{1,0:T(8,128)(2,1)S(1)}, f32[2,32,256]{2,1,0:T(8,128)S(1)}) custom-call(bf16[256,4096]{1,0:T(8,128)(2,1)} %bitcast.8, s32[32,256]{1,0:T(8,128)} %bitcast.10, bf16[256,4096]{1,0:T(8,128)(2,1)} %bitcast.9, s32[1,256]{1,0:T(1,128)} %bitcast.11, s32[1,256]{1,0:T(1,128)} %bitcast.12), custom_call_target="tpu_custom_call" | custom-call | tf_op jit(solution)/shard_map/gather/pallas_call | solution.py:413
  49.5 3.1 %fisher.1 = (f32[1,1024,1024]{2,1,0:T(8,128)}, f32[2,32,256]{2,1,0:T(8,128)}) custom-call(f32[1024,1024]{1,0:T(8,128)S(1)} %get-tuple-element.8.acc, bf16[256,1024]{1,0:T(8,128)(2,1)S(1)} %get-tuple-element.9.col, bf16[256,1024]{1,0:T(8,128)(2,1)S(1)} %get-tuple-element.10.own, f32[2,32,256]{2,1,0:T(8,128)S(1)} %get-tuple-element.11.ds_in), custom_call_target="tpu_custom_call" | custom-call | tf_op jit(solution)/shard_map/fisher/pallas_call | solution.py:466

commit v3 on v2

--- a/solution.py
+++ b/solution.py
@@ -28,11 +28,11 @@
 
 def gather_kernel(
     sizes, m_hbm, e_hbm, q_hbm, doc_hbm, owner_hbm,
-    acc_out, col_out, own_out, ds_out,
-    gcol, gown, ecol, eown, dcol, down, acc,
+    acc, col_out, own_out, ds_out,
+    gcol, gown, ecol, eown, dcol, down,
     mv, qv, ev, doc_ref, owner_ref, terms, from_layers, part, from_dp, total,
-    load_sem, l_sem, z_send, z_recv, o_send, o_recv, e_send, e_recv, f_send, f_recv,
-    x_send, x_recv, s_send, s_recv, r_send, r_recv, out_sem,
+    load_sem, z_send, z_recv, o_send, o_recv, e_send, e_recv, f_send, f_recv,
+    x_send, x_recv, s_send, s_recv, r_send, r_recv,
 ):
     n, layers, queries, pieces, own_width = sizes
     rows, width = m_hbm.shape
@@ -90,22 +90,22 @@
     def incoming(way, step):
         return d - 1 - step if way == 0 else d + 1 + step
 
+    e_rows = pl.ds(pl.multiple_of(q * col_blocks, 8), col_blocks)
+
+    def e_copy(step):
+        return remote(
+            e_hbm.at[e_rows], ecol.at[d], e_send.at[step - 1], e_recv.at[step - 1],
+            dp=other(d, step, n),
+        )
+
+    for step in range(1, n):
+        e_copy(step).start()
+
     for c in range(pieces):
         for way in (0, 1):
             @pl.when(sends(way, 0))
             def _(way=way, c=c):
                 z_copy(way, 0, c, True).start()
-
-    e_rows = pl.ds(pl.multiple_of(q * col_blocks, 8), col_blocks)
-
-    def e_copy(step):
-        return remote(
-            e_hbm.at[e_rows], ecol.at[d], e_send.at[step - 1], e_recv.at[step - 1],
-            dp=other(d, step, n),
-        )
-
-    for step in range(1, n):
-        e_copy(step).start()
 
     for load in loads:
         load.wait()
@@ -252,14 +252,6 @@
 
     last = jnp.where(d >= (n + 1) // 2, 0, n - 1)
     own_blocks = own_width // LANES
-    acc_copy = pltpu.make_async_copy(acc, acc_out, l_sem.at[0, 0])
-
-    def last_copies(way, c):
-        at = pl.ds(c * piece, piece)
-        return (
-            pltpu.make_async_copy(dcol.at[way, at], col_out.at[at], l_sem.at[1, c]),
-            pltpu.make_async_copy(down.at[way, at], own_out.at[at], l_sem.at[2, c]),
-        )
 
     def on_own(way, step, c):
         @pl.when(arrives(way, step))
@@ -304,8 +296,8 @@
 
             @pl.when(block == last)
             def _():
-                for copy in last_copies(way, c):
-                    copy.start()
+                col_out[at] = dcol[way, at]
+                own_out[at] = down[way, at]
 
             if c == pieces - 1:
                 @pl.when(block != last)
@@ -323,17 +315,15 @@
         if i >= lag:
             on_own(*items[i - lag])
         if i == 1:
+            exponents_on()
+        if i == 3:
             over_layers()
-        if i == 3:
-            exponents_on()
-        if i == 5:
+        if i == len(items) * 2 // 3:
             over_dp()
 
-    acc_copy.start()
     for step in range(1, layers):
         r_copy(step).wait_recv()
-    out = pltpu.make_async_copy(total, ds_out, out_sem)
-    out.start()
+    ds_out[...] = total[...]
 
     @pl.when(q == source)
     def _():
@@ -360,11 +350,6 @@
         @pl.when(jnp.logical_and(arrives(way, step), is_relay))
         def _(way=way, step=step, c=c):
             o_copy(way, step, c, 0, False).wait_send()
-    for c in range(pieces):
-        for copy in last_copies(0, c):
-            copy.wait()
-    acc_copy.wait()
-    out.wait()
 
 
 def fisher_kernel(scale, acc, col, own, ds_in, fisher, ds_out, tile, t_sem, ds_sem):
@@ -419,7 +404,7 @@
             pltpu.VMEM((layers, sub, count), f32),
         ),
         in_specs=[hbm] * 5,
-        out_specs=(anyspace,) * 4,
+        out_specs=(vmem, vmem, vmem, vmem),
         scratch_shapes=[
             pltpu.VMEM((n, rows, col_width), bf16),
             pltpu.VMEM((n, rows, own_width), bf16),
@@ -427,7 +412,6 @@
             pltpu.VMEM((n, col_blocks, rows), jnp.int32),
             pltpu.VMEM((2, rows, col_width), bf16),
             pltpu.VMEM((2, rows, own_width), bf16),
-            pltpu.VMEM((own_width, col_width), f32),
             pltpu.VMEM((rows, width), bf16),
             pltpu.VMEM((count, width), bf16),
             pltpu.VMEM(e.shape, jnp.int32),
@@ -439,7 +423,6 @@
             pltpu.VMEM((n - 1, sub, count), f32),
             pltpu.VMEM((layers, sub, count), f32),
             dma((5,)),
-            dma((3, pieces)),
             dma((2, n - 1, pieces)),
             dma((2, n - 1, pieces)),
             dma((2, n - 1, pieces, nq // 2)),
@@ -454,14 +437,13 @@
             dma((n - 1,)),
             dma((layers - 1,)),
             dma((layers - 1,)),
-            dma,
         ],
         compiler_params=pltpu.CompilerParams(
             collective_id=0, has_side_effects=True, vmem_limit_bytes=58 * 2**20
         ),
         name="gather",
     )(m, e, qs, doc_ids.reshape(1, rows), owners.reshape(1, docs))
-    height = min(128, own_width)
+    height = min(256, own_width)
     steps = own_width // height
     fisher, ds = pl.pallas_call(
         functools.partial(fisher_kernel, 1.0 / (n * rows)),

time: 52.8 us -> 51.2 us (0.970)
  Pallas kernels: 52 us -> 50.4 us
    pallas_call x1, Pallas kernels: 48.9 us -> 48 us  [per_device(): pl.pallas_call(functools.partial(gather_kernel, (n, layers, nq, pieces, o...]
    pallas_call x1, Pallas kernels: 3.05 us -> 2.39 us  [per_device(): pl.pallas_call(functools.partial(fisher_kernel, 1.0 / (n * rows)), out_sh...]
where the time goes in v3:
time: 51.2 us; the launch traced here: 51 us
  Pallas kernels  50.4 us (98%)
  between operations  0.64 us (1%)
    pallas_call x1, Pallas kernels, per_device(): pl.pallas_call(functools.partial(gather_kernel, (n, layers, nq, pieces, o...  48 us
    pallas_call x1, Pallas kernels, per_device(): pl.pallas_call(functools.partial(fisher_kernel, 1.0 / (n * rows)), out_sh...  2.39 us

profile of v3, /device:TPU:5, one launch (start us, length us, event | category | flops | bytes accessed | tf_op | source)
XLA Modules:
  0.0 51.0 jit_solution(17470535618865594045)
XLA Ops:
  0.6 48.0 %gather.1 = (f32[1024,1024]{1,0:T(8,128)S(1)}, bf16[256,1024]{1,0:T(8,128)(2,1)S(1)}, bf16[256,1024]{1,0:T(8,128)(2,1)S(1)}, f32[2,32,256]{2,1,0:T(8,128)S(1)}) custom-call(bf16[256,4096]{1,0:T(8,128)(2,1)} %bitcast.8, s32[32,256]{1,0:T(8,128)} %bitcast.10, bf16[256,4096]{1,0:T(8,128)(2,1)} %bitcast.9, s32[1,256]{1,0:T(1,128)} %bitcast.11, s32[1,256]{1,0:T(1,128)} %bitcast.12), custom_call_target="tpu_custom_call" | custom-call | tf_op jit(solution)/shard_map/gather/pallas_call | solution.py:398
  48.6 2.4 %fisher.1 = (f32[1,1024,1024]{2,1,0:T(8,128)}, f32[2,32,256]{2,1,0:T(8,128)}) custom-call(f32[1024,1024]{1,0:T(8,128)S(1)} %get-tuple-element.8.acc, bf16[256,1024]{1,0:T(8,128)(2,1)S(1)} %get-tuple-element.9.col, bf16[256,1024]{1,0:T(8,128)(2,1)S(1)} %get-tuple-element.10.own, f32[2,32,256]{2,1,0:T(8,128)S(1)} %get-tuple-element.11.ds_in), custom_call_target="tpu_custom_call" | custom-call | tf_op jit(solution)/shard_map/fisher/pallas_call | solution.py:448
